TPU v7x, 32 devices: a whole 2x2x4 slice. The times are simulated.
32 devices in a mesh: gx: 2 (over x), gy: 4 (over z), gz: 4 (over y, core).
Axes of the slice: x: 2, y: 2, z: 4, core: 2. Of those that a mesh axis runs over, the one named last changes fastest.
Arguments:
- source_field: float32 [3, 16, 32, 512], P(None, 'gx', 'gy', 'gz'), may hold values from -6 to 6
- cell_contrast: bfloat16 [4096, 1536], P(('gx', 'gy', 'gz')), may hold values from 0.19921875 to 2
- point_field: bfloat16 [3, 4096], P(None, ('gx', 'gy', 'gz')), may hold values from -3 to 3
- point_class: int32 [4096, 1], P(('gx', 'gy', 'gz')), may hold values from 0 to 1; in each aligned block of 128 rows (0 to 127, 128 to 255, ...) at most 128 rows name the same one
- cell_kind: int32 [4096], P(('gx', 'gy', 'gz')), may hold values from 0 to 3
- inverse_blocks: float32 [2, 4, 3, 3, 512], P('gx'), may hold values from -0.3 to 0.3
Outputs:
- newton_step: float32 [3, 16, 32, 512], P(None, 'gx', 'gy', 'gz')
- krylov_residual: float32 [3, 16, 32, 512], P(None, 'gx', 'gy', 'gz')
Inputs may be any that keep to these rules, and one draw needn't show every extreme that they name: `point_class`: among the 128 points of one device's block no class is named more than 128 times, a bound that some block reaches there.
All inputs are finite; a program needn't handle non-finite values.
Results may differ from a plain program's by a relative error of at most 0.0076.
Values may be sent and summed in bfloat16 or wider, within the bound.
No kernel may reach another device: no remote copies, remote signals or barrier semaphores. Data moves between devices by JAX's collectives and lax.ppermute only.
A program may use at most 64 MiB of HBM per device.

v0:
```python
import math
import jax
import jax.numpy as jnp
from jax import lax
from jax.sharding import PartitionSpec as P

CELL = 8
VOX = 512
TYPES = 4
ZP = 8
ITERS = 3
kerr_scale = 0.1


def with_halo(block, sides, width):
    for axis, dim in sides:
        count = lax.axis_size(axis)
        forward = [(i, i + 1) for i in range(count - 1)]
        backward = [(target, source) for source, target in forward]
        low = lax.ppermute(
            lax.slice_in_dim(block, block.shape[dim] - width, None, axis=dim), axis, forward
        )
        high = lax.ppermute(lax.slice_in_dim(block, 0, width, axis=dim), axis, backward)
        block = jnp.concatenate([low, block, high], axis=dim)
    return block


def hartley_table():
    voxel_index = jnp.arange(VOX, dtype=jnp.int32)
    along_one = voxel_index // (CELL * CELL)
    along_two = voxel_index // CELL % CELL
    along_three = voxel_index % CELL
    phase_index = (
        along_one[:, None] * along_one[None, :]
        + along_two[:, None] * along_two[None, :]
        + along_three[:, None] * along_three[None, :]
    ) % CELL
    phase_angle = 2.0 * math.pi / CELL * phase_index.astype(jnp.float32)
    return ((jnp.cos(phase_angle) + jnp.sin(phase_angle)) / math.sqrt(VOX)).astype(jnp.bfloat16)


def cell_solve(contrast, point_values, blocks, hartley):
    row_count = contrast.shape[0]
    weights = contrast.reshape(row_count, 3, VOX).astype(jnp.float32)
    base_field = point_values.astype(jnp.float32)[:, :, None]

    def correction(polarization):
        spectrum = jnp.dot(
            polarization.reshape(row_count * 3, VOX), hartley, preferred_element_type=jnp.float32
        ).reshape(row_count, 3, VOX)
        mixed_spectrum = jnp.sum(blocks * spectrum[:, None, :, :], axis=2).astype(jnp.bfloat16)
        return jnp.dot(
            mixed_spectrum.reshape(row_count * 3, VOX), hartley, preferred_element_type=jnp.float32
        ).reshape(row_count, 3, VOX)

    local_field = base_field - correction((weights * base_field).astype(jnp.bfloat16))
    kerr_polar = (weights * local_field * (1.0 + kerr_scale * local_field * local_field)).astype(
        jnp.bfloat16
    )
    final_field = base_field - correction(kerr_polar)
    flux_mean = jnp.mean((1.0 + weights) * final_field, axis=2)
    stiffness = 0.5 + jnp.mean(weights * final_field * final_field, axis=(1, 2))
    return jnp.concatenate([flux_mean, stiffness[:, None]], axis=1)


def solve_batched(contrast, point_values, keys, library, hartley):
    return cell_solve(contrast, point_values, library[keys], hartley)


def operate(field, diagonal):
    padded = with_halo(field, (("gx", 1), ("gy", 2), ("gz", 3)), 1)
    beside = padded[:, 2:, 1:-1, 1:-1] + padded[:, :-2, 1:-1, 1:-1]
    beside = beside + padded[:, 1:-1, 2:, 1:-1] + padded[:, 1:-1, :-2, 1:-1]
    beside = beside + padded[:, 1:-1, 1:-1, 2:] + padded[:, 1:-1, 1:-1, :-2]
    return (6.0 + diagonal)[None] * field - beside


def two_products(residual, image):
    return lax.psum((jnp.sum(residual * residual), jnp.sum(residual * image)), ("gx", "gy", "gz"))


def per_device(source_field, cell_contrast, point_field, point_class, cell_kind, inverse_blocks):
    hartley = hartley_table()
    point_values = point_field.T
    library = lax.all_gather(inverse_blocks, "gx", axis=0, tiled=True)
    library = library.reshape(library.shape[0] * library.shape[1], 3, 3, VOX)
    chosen = point_class[:, 0] * TYPES + cell_kind
    summary = solve_batched(cell_contrast, point_values, chosen, library, hartley)
    extent_x = source_field.shape[1]
    extent_y = source_field.shape[2]
    extent_z = source_field.shape[3]
    blocks_z = extent_z // ZP
    stiffness_grid = jnp.broadcast_to(
        summary[:, 3].reshape(1, extent_y, blocks_z, 1), (extent_x, extent_y, blocks_z, ZP)
    ).reshape(extent_x, extent_y, extent_z)
    flux_grid = jnp.broadcast_to(
        summary[:, :3].T.reshape(3, 1, extent_y, blocks_z, 1), (3, extent_x, extent_y, blocks_z, ZP)
    ).reshape(3, extent_x, extent_y, extent_z)
    right = source_field - flux_grid
    newton_step = jnp.zeros_like(right)
    residual = right
    image = operate(residual, stiffness_grid)
    norm_now, product = two_products(residual, image)
    alpha = norm_now / product
    direction, along = (residual, image)
    for iteration in range(ITERS):
        newton_step = newton_step + alpha * direction
        residual = residual - alpha * along
        if iteration + 1 < ITERS:
            image = operate(residual, stiffness_grid)
            norm_next, product = two_products(residual, image)
            ratio = norm_next / norm_now
            alpha = norm_next / (product - ratio * norm_next / alpha)
            direction = residual + ratio * direction
            along = image + ratio * along
            norm_now = norm_next
    return (newton_step, residual)


def solution(mesh):
    placed = (
        P(None, "gx", "gy", "gz"),
        P(("gx", "gy", "gz"), None),
        P(None, ("gx", "gy", "gz")),
        P(("gx", "gy", "gz"), None),
        P(("gx", "gy", "gz")),
        P("gx", None, None, None, None),
    )
    return jax.shard_map(
        per_device,
        mesh=mesh,
        in_specs=placed,
        out_specs=(P(None, "gx", "gy", "gz"), P(None, "gx", "gy", "gz")),
        check_vma=False,
    )
```

profile of v0, /device:TPU:0, one launch (start us, length us, event | category | flops | bytes accessed | tf_op | source)
XLA Modules:
  0.0 260.3 jit_solution(5146362177927208598)
XLA Ops:
  0.7 0.7 convert_bitcast_fusion
  1.3 0.7 compare_select_fusion
  2.0 6.2 %all_gather.3 = f32[2,4,3,3,512]{4,1,3,2,0:T(4,128)S(1)} all-gather(f32[1,4,3,3,512]{4,1,3,2,0:T(4,128)} %param.11), channel_id=1, replica_groups=mesh['gx'=2,'gy'=4,'gz'=4] {'gx'}, dimensions={0}, use_global_device_ids=true | all-gather | bytes 221184 | tf_op jit(solution)/shard_map/all_gather | solution.py:85
  8.2 0.1 copy.45
  8.3 1.2 copy.34
  9.6 0.2 copy.35
  9.8 4.7 %fusion.12 = f32[128,3,512]{2,0,1:T(8,128)S(1)} fusion(s32[512]{0:T(512)S(1)} %get-tuple-element.39, s32[512]{0:T(512)S(1)} %get-tuple-element.40, s32[512]{0:T(512)S(1)} %add_select_fusion.4, f32[128,3,512]{2,0,1:T(8,128)S(1)} %copy.35, f32[128,3]{0,1:T(4,128)S(1)} %convert_bitcast_fusion), kind=kOutput, calls=%fused_computation.24 | convolution fusion | flops 207224832 | bytes 1580544 | tf_op jit(solution)/shard_map/dot_general | solution.py:48
  14.5 1.5 copy.39
  16.0 2.4 gather_fusion
  18.5 4.6 %multiply_reduce_fusion.1 = bf16[128,3,512]{2,1,0:T(4,128)(2,1)} fusion(f32[128,3,3,512]{3,2,1,0:T(4,128)S(1)} %gather_fusion, f32[128,3,512]{2,1,0:T(4,128)} %copy.39), kind=kLoop, calls=%fused_computation.2 | loop fusion | flops 983040 | bytes 3538944 | tf_op jit(solution)/shard_map/reduce_sum | solution.py:51
  23.1 11.6 %fusion.7 = f32[128,3,512]{2,0,1:T(8,128)} fusion(f32[128,3,512]{2,0,1:T(8,128)} %copy-done.1, s32[512]{0:T(512)S(1)} %get-tuple-element.39, s32[512]{0:T(512)S(1)} %get-tuple-element.40, s32[512]{0:T(512)S(1)} %add_select_fusion.4, bf16[128,3,512]{2,1,0:T(4,128)(2,1)} %multiply_reduce_fusion.1, f32[128,3]{0,1:T(4,128)S(1)} %convert_bitcast_fusion), kind=kOutput, calls=%fused_computation.21 | convolution fusion | flops 415039488 | bytes 1973760 | tf_op jit(solution)/shard_map/dot_general | solution.py:48
  34.7 1.7 copy.42
  36.5 3.5 %multiply_reduce_fusion = bf16[128,3,512]{2,1,0:T(4,128)(2,1)S(1)} fusion(f32[128,3,3,512]{3,2,1,0:T(4,128)S(1)} %gather_fusion, f32[128,3,512]{2,1,0:T(4,128)S(1)} %copy.42), kind=kLoop, calls=%fused_computation.1 | loop fusion | flops 983040 | bytes 3538944 | tf_op jit(solution)/shard_map/reduce_sum | solution.py:51
  39.9 5.2 %fusion.6 = (f32[128]{0:T(128)S(1)}, f32[128,3]{0,1:T(4,128)S(1)}) fusion(f32[128,3,512]{2,0,1:T(8,128)S(1)} %copy-done.2, s32[512]{0:T(512)S(1)} %get-tuple-element.39, s32[512]{0:T(512)S(1)} %get-tuple-element.40, s32[512]{0:T(512)S(1)} %add_select_fusion.4, bf16[128,3,512]{2,1,0:T(4,128)(2,1)S(1)} %multiply_reduce_fusion, ...), kind=kOutput, calls=%fused_computation.17 | convolution fusion | flops 208207360 | bytes 1189376 | tf_op jit(solution)/shard_map/dot_general | solution.py:52
  45.1 0.1 broadcast_in_dim.13
  45.2 0.1 broadcast_in_dim.14
  45.3 0.1 broadcast_in_dim.15
  45.5 3.9 %collective-permute-start.1 = (f32[3,1,8,128]{3,2,1,0:T(8,128)S(1)}, f32[3,1,8,128]{3,2,1,0:T(8,128)S(1)}, u32[]{:S(2)}, u32[]{:S(2)}) collective-permute-start(f32[3,1,8,128]{3,2,1,0:T(8,128)S(1)} %get-tuple-element.37), channel_id=1, source_target_pairs={{0,16},{1,17},{2,18},{3,19},{4,20},{5,21},{6,22},{7,23},{8,24},{9,... | collective-permute-start | bytes 36872 | tf_op jit(solution)/shard_map/ppermute | solution.py:20
  49.4 1.3 collective-permute-start
  50.7 0.1 collective-permute-done.1
  50.8 4.2 %collective-permute-done = f32[3,1,8,128]{3,2,1,0:T(8,128)S(1)} collective-permute-done((f32[3,1,8,128]{3,2,1,0:T(8,128)S(1)}, f32[3,1,8,128]{3,2,1,0:T(8,128)S(1)}, u32[]{:S(2)}, u32[]{:S(2)}) %collective-permute-start) | collective-permute-done | bytes 12320 | tf_op jit(solution)/shard_map/ppermute | solution.py:23
  55.0 3.5 %collective-permute-start.3 = (f32[3,10,1,128]{3,2,1,0:T(1,128)S(1)}, f32[3,10,1,128]{3,2,1,0:T(1,128)S(1)}, u32[]{:S(2)}, u32[]{:S(2)}) collective-permute-start(f32[3,10,1,128]{3,2,1,0:T(1,128)S(1)} %get-tuple-element.29), channel_id=1, source_target_pairs={{0,4},{4,8},{8,12},{1,5},{5,9},{9,13},{2,6},{6,10},{10,14},{3,7},{... | collective-permute-start | bytes 46088 | tf_op jit(solution)/shard_map/ppermute | solution.py:20
  58.5 1.3 collective-permute-start.2
  59.8 0.1 collective-permute-done.3
  59.9 4.2 %collective-permute-done.2 = f32[3,10,1,128]{3,2,1,0:T(1,128)S(1)} collective-permute-done((f32[3,10,1,128]{3,2,1,0:T(1,128)S(1)}, f32[3,10,1,128]{3,2,1,0:T(1,128)S(1)}, u32[]{:S(2)}, u32[]{:S(2)}) %collective-permute-start.2) | collective-permute-done | bytes 15392 | tf_op jit(solution)/shard_map/ppermute | solution.py:23
  64.1 0.1 pad_maximum_fusion
  64.1 0.1 fusion.70
  64.3 1.3 collective-permute-start.4
  65.6 3.0 %collective-permute-start.5 = (f32[3,10,10,1]{3,2,1,0:T(8,128)S(1)}, f32[3,10,10,1]{3,2,1,0:T(8,128)S(1)}, u32[]{:S(2)}, u32[]{:S(2)}) collective-permute-start(f32[3,10,10,1]{3,2,1,0:T(8,128)S(1)} %get-tuple-element.24), channel_id=1, source_target_pairs={{0,1},{1,2},{2,3},{4,5},{5,6},{6,7},{8,9},{9,10},{10,11},{12,13},{... | collective-permute-start | bytes 3608 | tf_op jit(solution)/shard_map/ppermute | solution.py:20
  68.6 0.1 add.222
  68.7 0.1 broadcast_in_dim.34
  68.8 0.1 add.223
  68.9 0.8 collective-permute-done.5
  69.7 0.8 multiply_reduce_fusion.7
  70.5 43.3 %all-reduce.2 = (f32[]{:T(128)}, f32[]{:T(128)}) all-reduce(f32[]{:T(128)} %get-tuple-element.9, f32[]{:T(128)} %get-tuple-element.8), channel_id=1, replica_groups=mesh['gx'=2,'gy'=4,'gz'=4] {'gx','gy','gz'}, use_global_device_ids=true, to_apply=%region_4.5 | all-reduce | flops 2 | bytes 16 | tf_op jit(solution)/shard_map/psum | solution.py:79
  115.2 4.2 %collective-permute-start.7 = (f32[3,1,8,128]{3,2,1,0:T(8,128)S(1)}, f32[3,1,8,128]{3,2,1,0:T(8,128)S(1)}, u32[]{:S(2)}, u32[]{:S(2)}) collective-permute-start(f32[3,1,8,128]{3,2,1,0:T(8,128)S(1)} %get-tuple-element.35), channel_id=1, source_target_pairs={{0,16},{1,17},{2,18},{3,19},{4,20},{5,21},{6,22},{7,23},{8,24},{9,... | collective-permute-start | bytes 36872 | tf_op jit(solution)/shard_map/ppermute | solution.py:20
  119.4 1.3 collective-permute-start.6
  120.7 0.1 collective-permute-done.7
  120.7 4.2 %collective-permute-done.6 = f32[3,1,8,128]{3,2,1,0:T(8,128)S(1)} collective-permute-done((f32[3,1,8,128]{3,2,1,0:T(8,128)S(1)}, f32[3,1,8,128]{3,2,1,0:T(8,128)S(1)}, u32[]{:S(2)}, u32[]{:S(2)}) %collective-permute-start.6) | collective-permute-done | bytes 12320 | tf_op jit(solution)/shard_map/ppermute | solution.py:23
  125.0 2.1 collective-permute-start.9
  127.1 1.3 collective-permute-start.8
  128.4 0.1 collective-permute-done.9
  128.5 4.2 %collective-permute-done.8 = f32[3,10,1,128]{3,2,1,0:T(1,128)S(1)} collective-permute-done((f32[3,10,1,128]{3,2,1,0:T(1,128)S(1)}, f32[3,10,1,128]{3,2,1,0:T(1,128)S(1)}, u32[]{:S(2)}, u32[]{:S(2)}) %collective-permute-start.8) | collective-permute-done | bytes 15392 | tf_op jit(solution)/shard_map/ppermute | solution.py:23
  132.7 0.1 fusion.69
  132.9 1.3 collective-permute-start.10
  134.2 3.0 %collective-permute-start.11 = (f32[3,10,10,1]{3,2,1,0:T(8,128)S(1)}, f32[3,10,10,1]{3,2,1,0:T(8,128)S(1)}, u32[]{:S(2)}, u32[]{:S(2)}) collective-permute-start(f32[3,10,10,1]{3,2,1,0:T(8,128)S(1)} %get-tuple-element.22), channel_id=1, source_target_pairs={{0,1},{1,2},{2,3},{4,5},{5,6},{6,7},{8,9},{9,10},{10,11},{12,13},{... | collective-permute-start | bytes 3608 | tf_op jit(solution)/shard_map/ppermute | solution.py:20
  137.2 1.1 collective-permute-done.11
  138.3 0.8 multiply_reduce_fusion.5
  139.2 43.9 %all-reduce.1 = (f32[]{:T(128)}, f32[]{:T(128)}) all-reduce(f32[]{:T(128)} %get-tuple-element.7, f32[]{:T(128)} %get-tuple-element.6), channel_id=1, replica_groups=mesh['gx'=2,'gy'=4,'gz'=4] {'gx','gy','gz'}, use_global_device_ids=true, to_apply=%region_9.10 | all-reduce | flops 2 | bytes 16 | tf_op jit(solution)/shard_map/psum | solution.py:79
  187.6 4.2 %collective-permute-start.13 = (f32[3,1,8,128]{3,2,1,0:T(8,128)S(1)}, f32[3,1,8,128]{3,2,1,0:T(8,128)S(1)}, u32[]{:S(2)}, u32[]{:S(2)}) collective-permute-start(f32[3,1,8,128]{3,2,1,0:T(8,128)S(1)} %get-tuple-element.33), channel_id=1, source_target_pairs={{0,16},{1,17},{2,18},{3,19},{4,20},{5,21},{6,22},{7,23},{8,24},{9,... | collective-permute-start | bytes 36872 | tf_op jit(solution)/shard_map/ppermute | solution.py:20
  191.8 1.3 collective-permute-start.12
  193.1 0.1 collective-permute-done.13
  193.2 4.2 %collective-permute-done.12 = f32[3,1,8,128]{3,2,1,0:T(8,128)S(1)} collective-permute-done((f32[3,1,8,128]{3,2,1,0:T(8,128)S(1)}, f32[3,1,8,128]{3,2,1,0:T(8,128)S(1)}, u32[]{:S(2)}, u32[]{:S(2)}) %collective-permute-start.12) | collective-permute-done | bytes 12320 | tf_op jit(solution)/shard_map/ppermute | solution.py:23
  197.4 2.1 collective-permute-start.15
  199.5 1.3 collective-permute-start.14
  200.8 0.1 collective-permute-done.15
  200.9 4.2 %collective-permute-done.14 = f32[3,10,1,128]{3,2,1,0:T(1,128)S(1)} collective-permute-done((f32[3,10,1,128]{3,2,1,0:T(1,128)S(1)}, f32[3,10,1,128]{3,2,1,0:T(1,128)S(1)}, u32[]{:S(2)}, u32[]{:S(2)}) %collective-permute-start.14) | collective-permute-done | bytes 15392 | tf_op jit(solution)/shard_map/ppermute | solution.py:23
  205.2 0.1 fusion.68
  205.3 1.3 collective-permute-start.16
  206.6 3.0 %collective-permute-start.17 = (f32[3,10,10,1]{3,2,1,0:T(8,128)S(1)}, f32[3,10,10,1]{3,2,1,0:T(8,128)S(1)}, u32[]{:S(2)}, u32[]{:S(2)}) collective-permute-start(f32[3,10,10,1]{3,2,1,0:T(8,128)S(1)} %get-tuple-element.20), channel_id=1, source_target_pairs={{0,1},{1,2},{2,3},{4,5},{5,6},{6,7},{8,9},{9,10},{10,11},{12,13},{... | collective-permute-start | bytes 3608 | tf_op jit(solution)/shard_map/ppermute | solution.py:20
  209.7 1.1 collective-permute-done.17
  210.8 0.8 multiply_reduce_fusion.3
  211.6 44.0 %all-reduce = (f32[]{:T(128)}, f32[]{:T(128)}) all-reduce(f32[]{:T(128)} %get-tuple-element.5, f32[]{:T(128)} %get-tuple-element.4), channel_id=1, replica_groups=mesh['gx'=2,'gy'=4,'gz'=4] {'gx','gy','gz'}, use_global_device_ids=true, to_apply=%region_13.14 | all-reduce | flops 2 | bytes 16 | tf_op jit(solution)/shard_map/psum | solution.py:79
  259.5 0.7 multiply_subtract_fusion
  (25 shorter events, 0.3 us)
Async XLA Ops:
  9.7 4.8 %copy-start.1 = (f32[128,3,512]{2,0,1:T(8,128)}, f32[128,3,512]{2,0,1:T(8,128)S(1)}, u32[]{:S(2)}) copy-start(f32[128,3,512]{2,0,1:T(8,128)S(1)} %copy.35) | copy-start | bytes 2359300
  34.7 5.2 %copy-start.2 = (f32[128,3,512]{2,0,1:T(8,128)S(1)}, f32[128,3,512]{2,0,1:T(8,128)}, u32[]{:S(2)}) copy-start(f32[128,3,512]{2,0,1:T(8,128)} %copy-done.1) | copy-start | bytes 2359300
  39.9 5.5 %copy-start = (f32[3,8,8,128]{3,2,1,0:T(8,128)S(1)}, f32[3,8,8,128]{3,2,1,0:T(8,128)}, u32[]{:S(2)}) copy-start(f32[3,8,8,128]{3,2,1,0:T(8,128)} %param.6) | copy-start | bytes 294916
  45.5 5.3 %collective-permute-start.1 = (f32[3,1,8,128]{3,2,1,0:T(8,128)S(1)}, f32[3,1,8,128]{3,2,1,0:T(8,128)S(1)}, u32[]{:S(2)}, u32[]{:S(2)}) collective-permute-start(f32[3,1,8,128]{3,2,1,0:T(8,128)S(1)} %get-tuple-element.37), channel_id=1, source_target_pairs={{0,16},{1,17},{2,18},{3,19},{4,20},{5,21},{6,22},{7,23},{8,24},{9,... | collective-permute-start | bytes 36872 | tf_op jit(solution)/shard_map/ppermute | solution.py:20
  49.4 5.6 %collective-permute-start = (f32[3,1,8,128]{3,2,1,0:T(8,128)S(1)}, f32[3,1,8,128]{3,2,1,0:T(8,128)S(1)}, u32[]{:S(2)}, u32[]{:S(2)}) collective-permute-start(f32[3,1,8,128]{3,2,1,0:T(8,128)S(1)} %get-tuple-element.38), channel_id=1, source_target_pairs={{16,0},{17,1},{18,2},{19,3},{20,4},{21,5},{22,6},{23,7},{24,8},{25... | collective-permute-start | bytes 36872 | tf_op jit(solution)/shard_map/ppermute | solution.py:23
  55.0 4.9 %collective-permute-start.3 = (f32[3,10,1,128]{3,2,1,0:T(1,128)S(1)}, f32[3,10,1,128]{3,2,1,0:T(1,128)S(1)}, u32[]{:S(2)}, u32[]{:S(2)}) collective-permute-start(f32[3,10,1,128]{3,2,1,0:T(1,128)S(1)} %get-tuple-element.29), channel_id=1, source_target_pairs={{0,4},{4,8},{8,12},{1,5},{5,9},{9,13},{2,6},{6,10},{10,14},{3,7},{... | collective-permute-start | bytes 46088 | tf_op jit(solution)/shard_map/ppermute | solution.py:20
  58.5 5.6 %collective-permute-start.2 = (f32[3,10,1,128]{3,2,1,0:T(1,128)S(1)}, f32[3,10,1,128]{3,2,1,0:T(1,128)S(1)}, u32[]{:S(2)}, u32[]{:S(2)}) collective-permute-start(f32[3,10,1,128]{3,2,1,0:T(1,128)S(1)} %get-tuple-element.30), channel_id=1, source_target_pairs={{4,0},{8,4},{12,8},{5,1},{9,5},{13,9},{6,2},{10,6},{14,10},{7,3},{... | collective-permute-start | bytes 46088 | tf_op jit(solution)/shard_map/ppermute | solution.py:23
  64.3 4.6 %collective-permute-start.4 = (f32[3,10,10,1]{3,2,1,0:T(8,128)S(1)}, f32[3,10,10,1]{3,2,1,0:T(8,128)S(1)}, u32[]{:S(2)}, u32[]{:S(2)}) collective-permute-start(f32[3,10,10,1]{3,2,1,0:T(8,128)S(1)} %get-tuple-element.23), channel_id=1, source_target_pairs={{1,0},{2,1},{3,2},{5,4},{6,5},{7,6},{9,8},{10,9},{11,10},{13,12},{... | collective-permute-start | bytes 3608 | tf_op jit(solution)/shard_map/ppermute | solution.py:23
  65.6 4.2 %collective-permute-start.5 = (f32[3,10,10,1]{3,2,1,0:T(8,128)S(1)}, f32[3,10,10,1]{3,2,1,0:T(8,128)S(1)}, u32[]{:S(2)}, u32[]{:S(2)}) collective-permute-start(f32[3,10,10,1]{3,2,1,0:T(8,128)S(1)} %get-tuple-element.24), channel_id=1, source_target_pairs={{0,1},{1,2},{2,3},{4,5},{5,6},{6,7},{8,9},{9,10},{10,11},{12,13},{... | collective-permute-start | bytes 3608 | tf_op jit(solution)/shard_map/ppermute | solution.py:20
  115.2 5.6 %collective-permute-start.7 = (f32[3,1,8,128]{3,2,1,0:T(8,128)S(1)}, f32[3,1,8,128]{3,2,1,0:T(8,128)S(1)}, u32[]{:S(2)}, u32[]{:S(2)}) collective-permute-start(f32[3,1,8,128]{3,2,1,0:T(8,128)S(1)} %get-tuple-element.35), channel_id=1, source_target_pairs={{0,16},{1,17},{2,18},{3,19},{4,20},{5,21},{6,22},{7,23},{8,24},{9,... | collective-permute-start | bytes 36872 | tf_op jit(solution)/shard_map/ppermute | solution.py:20
  119.4 5.6 %collective-permute-start.6 = (f32[3,1,8,128]{3,2,1,0:T(8,128)S(1)}, f32[3,1,8,128]{3,2,1,0:T(8,128)S(1)}, u32[]{:S(2)}, u32[]{:S(2)}) collective-permute-start(f32[3,1,8,128]{3,2,1,0:T(8,128)S(1)} %get-tuple-element.36), channel_id=1, source_target_pairs={{16,0},{17,1},{18,2},{19,3},{20,4},{21,5},{22,6},{23,7},{24,8},{25... | collective-permute-start | bytes 36872 | tf_op jit(solution)/shard_map/ppermute | solution.py:23
  125.0 3.5 %collective-permute-start.9 = (f32[3,10,1,128]{3,2,1,0:T(1,128)S(1)}, f32[3,10,1,128]{3,2,1,0:T(1,128)S(1)}, u32[]{:S(2)}, u32[]{:S(2)}) collective-permute-start(f32[3,10,1,128]{3,2,1,0:T(1,128)S(1)} %get-tuple-element.27), channel_id=1, source_target_pairs={{0,4},{4,8},{8,12},{1,5},{5,9},{9,13},{2,6},{6,10},{10,14},{3,7},{... | collective-permute-start | bytes 46088 | tf_op jit(solution)/shard_map/ppermute | solution.py:20
  127.1 5.6 %collective-permute-start.8 = (f32[3,10,1,128]{3,2,1,0:T(1,128)S(1)}, f32[3,10,1,128]{3,2,1,0:T(1,128)S(1)}, u32[]{:S(2)}, u32[]{:S(2)}) collective-permute-start(f32[3,10,1,128]{3,2,1,0:T(1,128)S(1)} %get-tuple-element.28), channel_id=1, source_target_pairs={{4,0},{8,4},{12,8},{5,1},{9,5},{13,9},{6,2},{10,6},{14,10},{7,3},{... | collective-permute-start | bytes 46088 | tf_op jit(solution)/shard_map/ppermute | solution.py:23
  132.9 4.4 %collective-permute-start.10 = (f32[3,10,10,1]{3,2,1,0:T(8,128)S(1)}, f32[3,10,10,1]{3,2,1,0:T(8,128)S(1)}, u32[]{:S(2)}, u32[]{:S(2)}) collective-permute-start(f32[3,10,10,1]{3,2,1,0:T(8,128)S(1)} %get-tuple-element.21), channel_id=1, source_target_pairs={{1,0},{2,1},{3,2},{5,4},{6,5},{7,6},{9,8},{10,9},{11,10},{13,12},{... | collective-permute-start | bytes 3608 | tf_op jit(solution)/shard_map/ppermute | solution.py:23
  134.2 4.2 %collective-permute-start.11 = (f32[3,10,10,1]{3,2,1,0:T(8,128)S(1)}, f32[3,10,10,1]{3,2,1,0:T(8,128)S(1)}, u32[]{:S(2)}, u32[]{:S(2)}) collective-permute-start(f32[3,10,10,1]{3,2,1,0:T(8,128)S(1)} %get-tuple-element.22), channel_id=1, source_target_pairs={{0,1},{1,2},{2,3},{4,5},{5,6},{6,7},{8,9},{9,10},{10,11},{12,13},{... | collective-permute-start | bytes 3608 | tf_op jit(solution)/shard_map/ppermute | solution.py:20
  187.6 5.6 %collective-permute-start.13 = (f32[3,1,8,128]{3,2,1,0:T(8,128)S(1)}, f32[3,1,8,128]{3,2,1,0:T(8,128)S(1)}, u32[]{:S(2)}, u32[]{:S(2)}) collective-permute-start(f32[3,1,8,128]{3,2,1,0:T(8,128)S(1)} %get-tuple-element.33), channel_id=1, source_target_pairs={{0,16},{1,17},{2,18},{3,19},{4,20},{5,21},{6,22},{7,23},{8,24},{9,... | collective-permute-start | bytes 36872 | tf_op jit(solution)/shard_map/ppermute | solution.py:20
  191.8 5.6 %collective-permute-start.12 = (f32[3,1,8,128]{3,2,1,0:T(8,128)S(1)}, f32[3,1,8,128]{3,2,1,0:T(8,128)S(1)}, u32[]{:S(2)}, u32[]{:S(2)}) collective-permute-start(f32[3,1,8,128]{3,2,1,0:T(8,128)S(1)} %get-tuple-element.34), channel_id=1, source_target_pairs={{16,0},{17,1},{18,2},{19,3},{20,4},{21,5},{22,6},{23,7},{24,8},{25... | collective-permute-start | bytes 36872 | tf_op jit(solution)/shard_map/ppermute | solution.py:23
  197.4 3.5 %collective-permute-start.15 = (f32[3,10,1,128]{3,2,1,0:T(1,128)S(1)}, f32[3,10,1,128]{3,2,1,0:T(1,128)S(1)}, u32[]{:S(2)}, u32[]{:S(2)}) collective-permute-start(f32[3,10,1,128]{3,2,1,0:T(1,128)S(1)} %get-tuple-element.25), channel_id=1, source_target_pairs={{0,4},{4,8},{8,12},{1,5},{5,9},{9,13},{2,6},{6,10},{10,14},{3,7},{... | collective-permute-start | bytes 46088 | tf_op jit(solution)/shard_map/ppermute | solution.py:20
  199.5 5.6 %collective-permute-start.14 = (f32[3,10,1,128]{3,2,1,0:T(1,128)S(1)}, f32[3,10,1,128]{3,2,1,0:T(1,128)S(1)}, u32[]{:S(2)}, u32[]{:S(2)}) collective-permute-start(f32[3,10,1,128]{3,2,1,0:T(1,128)S(1)} %get-tuple-element.26), channel_id=1, source_target_pairs={{4,0},{8,4},{12,8},{5,1},{9,5},{13,9},{6,2},{10,6},{14,10},{7,3},{... | collective-permute-start | bytes 46088 | tf_op jit(solution)/shard_map/ppermute | solution.py:23
  205.3 4.4 %collective-permute-start.16 = (f32[3,10,10,1]{3,2,1,0:T(8,128)S(1)}, f32[3,10,10,1]{3,2,1,0:T(8,128)S(1)}, u32[]{:S(2)}, u32[]{:S(2)}) collective-permute-start(f32[3,10,10,1]{3,2,1,0:T(8,128)S(1)} %get-tuple-element.19), channel_id=1, source_target_pairs={{1,0},{2,1},{3,2},{5,4},{6,5},{7,6},{9,8},{10,9},{11,10},{13,12},{... | collective-permute-start | bytes 3608 | tf_op jit(solution)/shard_map/ppermute | solution.py:23
  206.6 4.2 %collective-permute-start.17 = (f32[3,10,10,1]{3,2,1,0:T(8,128)S(1)}, f32[3,10,10,1]{3,2,1,0:T(8,128)S(1)}, u32[]{:S(2)}, u32[]{:S(2)}) collective-permute-start(f32[3,10,10,1]{3,2,1,0:T(8,128)S(1)} %get-tuple-element.20), channel_id=1, source_target_pairs={{0,1},{1,2},{2,3},{4,5},{5,6},{6,7},{8,9},{9,10},{10,11},{12,13},{... | collective-permute-start | bytes 3608 | tf_op jit(solution)/shard_map/ppermute | solution.py:20
where the time goes:
time: 261 us; the launch traced here: 260 us
  blocking collectives  137 us (52%)
  starting transfers between devices  40.7 us (16%)
  waiting for transfers between devices  28.8 us (11%)
  matrix products  21.5 us (8%)
  other arithmetic  12.9 us (5%)
  between operations  10.8 us (4%)
  local copies, waits for them, and re-layouts  8.15 us (3%)
    psum x3, blocking collectives, two_products(): lax.psum((jnp.sum(residual * residual), jnp.sum(residual * image)), ('gx'...  131 us
    ppermute x9, starting transfers between devices, with_halo(): lax.ppermute(lax.slice_in_dim(block, block.shape[dim] - width, None, axis...  29 us
    ppermute x9, waiting for transfers between devices, with_halo(): lax.ppermute(lax.slice_in_dim(block, 0, width, axis=dim), axis, backward)  25.2 us
    dot_general x2, matrix products, correction(): jnp.dot(polarization.reshape(row_count * 3, VOX), hartley, preferred_elem...  16.4 us
    ppermute x9, starting transfers between devices, with_halo(): lax.ppermute(lax.slice_in_dim(block, 0, width, axis=dim), axis, backward)  11.6 us
    reduce_sum x2, other arithmetic, correction(): jnp.sum(blocks * spectrum[:, None, :, :], axis=2).astype(jnp.bfloat16)  8.07 us
    all_gather x1, blocking collectives, per_device(): library = lax.all_gather(inverse_blocks, 'gx', axis=0, tiled=True)  6.23 us
  transfers between devices with their start and end apart: 18, of which 15 were waited for; matrix products, arithmetic and copies ran while one was open for 0% of the time, Pallas kernels for 0%

commit v1 on v0

--- a/solution.py
+++ b/solution.py
@@ -76,7 +76,10 @@
 
 
 def two_products(residual, image):
-    return lax.psum((jnp.sum(residual * residual), jnp.sum(residual * image)), ("gx", "gy", "gz"))
+    return lax.psum(
+        lax.psum((jnp.sum(residual * residual), jnp.sum(residual * image)), axis_name=("gy", "gz")),
+        axis_name="gx",
+    )
 
 
 def per_device(source_field, cell_contrast, point_field, point_class, cell_kind, inverse_blocks):

time: 261 us -> 238 us (0.912)
  blocking collectives: 137 us -> 120 us
  starting transfers between devices: 40.7 us -> 34.5 us
    psum x3 -> x6, blocking collectives: 131 us -> 114 us  [the longest x3 97.6 us: two_products(): lax.psum((jnp.sum(residual * residual), jnp.sum(residual * image)), axis_...]
    ppermute x9, starting transfers between devices: 29 us -> 22.9 us  [with_halo(): lax.ppermute(lax.slice_in_dim(block, block.shape[dim] - width, None, axis...]
where the time goes in v1:
time: 238 us; the launch traced here: 237 us
  blocking collectives  120 us (50%)
  starting transfers between devices  34.5 us (14%)
  waiting for transfers between devices  28.8 us (12%)
  matrix products  21.5 us (9%)
  other arithmetic  12.9 us (5%)
  between operations  10.9 us (5%)
  local copies, waits for them, and re-layouts  8.16 us (3%)
    psum x3, blocking collectives, two_products(): lax.psum((jnp.sum(residual * residual), jnp.sum(residual * image)), axis_...  97.6 us
    ppermute x9, waiting for transfers between devices, with_halo(): lax.ppermute(lax.slice_in_dim(block, 0, width, axis=dim), axis, backward)  25.2 us
    ppermute x9, starting transfers between devices, with_halo(): lax.ppermute(lax.slice_in_dim(block, block.shape[dim] - width, None, axis...  22.9 us
    psum x3, blocking collectives, two_products(): lax.psum(lax.psum((jnp.sum(residual * residual), jnp.sum(residual * image...  16.7 us
    dot_general x2, matrix products, correction(): jnp.dot(polarization.reshape(row_count * 3, VOX), hartley, preferred_elem...  16.3 us
    ppermute x9, starting transfers between devices, with_halo(): lax.ppermute(lax.slice_in_dim(block, 0, width, axis=dim), axis, backward)  11.6 us
    reduce_sum x2, other arithmetic, correction(): jnp.sum(blocks * spectrum[:, None, :, :], axis=2).astype(jnp.bfloat16)  8.06 us
    all_gather x1, blocking collectives, per_device(): library = lax.all_gather(inverse_blocks, 'gx', axis=0, tiled=True)  6.23 us
  transfers between devices with their start and end apart: 18, of which 15 were waited for; matrix products, arithmetic and copies ran while one was open for 0% of the time, Pallas kernels for 0%

profile of v1, /device:TPU:0, one launch (start us, length us, event | category | flops | bytes accessed | tf_op | source)
XLA Modules:
  0.0 237.3 jit_solution(3420601430040013988)
XLA Ops:
  0.7 0.7 convert_bitcast_fusion
  1.3 0.7 compare_select_fusion
  2.0 6.2 %all_gather.3 = f32[2,4,3,3,512]{4,1,3,2,0:T(4,128)S(1)} all-gather(f32[1,4,3,3,512]{4,1,3,2,0:T(4,128)} %param.11), channel_id=1, replica_groups=mesh['gx'=2,'gy'=4,'gz'=4] {'gx'}, dimensions={0}, use_global_device_ids=true | all-gather | bytes 221184 | tf_op jit(solution)/shard_map/all_gather | solution.py:88
  8.2 0.1 copy.45
  8.3 1.2 copy.34
  9.6 0.2 copy.35
  9.8 4.7 %fusion.12 = f32[128,3,512]{2,0,1:T(8,128)S(1)} fusion(s32[512]{0:T(512)S(1)} %get-tuple-element.45, s32[512]{0:T(512)S(1)} %get-tuple-element.46, s32[512]{0:T(512)S(1)} %add_select_fusion.4, f32[128,3,512]{2,0,1:T(8,128)S(1)} %copy.35, f32[128,3]{0,1:T(4,128)S(1)} %convert_bitcast_fusion), kind=kOutput, calls=%fused_computation.24 | convolution fusion | flops 207224832 | bytes 1580544 | tf_op jit(solution)/shard_map/dot_general | solution.py:48
  14.5 1.5 copy.39
  16.0 2.4 %gather_fusion = f32[128,3,3,512]{3,2,1,0:T(4,128)S(1)} fusion(f32[8,3,3,512]{3,2,1,0:T(4,128)S(1)} %bitcast.21, s32[1024]{0:T(1024)S(1)} %pad_clamp_fusion), kind=kCustom, calls=%fused_computation | custom fusion | bytes 4719104 | tf_op jit(solution)/shard_map/gather | solution.py:67
  18.5 4.6 %multiply_reduce_fusion.1 = bf16[128,3,512]{2,1,0:T(4,128)(2,1)} fusion(f32[128,3,3,512]{3,2,1,0:T(4,128)S(1)} %gather_fusion, f32[128,3,512]{2,1,0:T(4,128)} %copy.39), kind=kLoop, calls=%fused_computation.2 | loop fusion | flops 983040 | bytes 3538944 | tf_op jit(solution)/shard_map/reduce_sum | solution.py:51
  23.1 11.6 %fusion.7 = f32[128,3,512]{2,0,1:T(8,128)} fusion(f32[128,3,512]{2,0,1:T(8,128)} %copy-done.1, s32[512]{0:T(512)S(1)} %get-tuple-element.45, s32[512]{0:T(512)S(1)} %get-tuple-element.46, s32[512]{0:T(512)S(1)} %add_select_fusion.4, bf16[128,3,512]{2,1,0:T(4,128)(2,1)} %multiply_reduce_fusion.1, f32[128,3]{0,1:T(4,128)S(1)} %convert_bitcast_fusion), kind=kOutput, calls=%fused_computation.21 | convolution fusion | flops 415039488 | bytes 1973760 | tf_op jit(solution)/shard_map/dot_general | solution.py:48
  34.7 1.7 copy.42
  36.4 3.5 %multiply_reduce_fusion = bf16[128,3,512]{2,1,0:T(4,128)(2,1)S(1)} fusion(f32[128,3,3,512]{3,2,1,0:T(4,128)S(1)} %gather_fusion, f32[128,3,512]{2,1,0:T(4,128)S(1)} %copy.42), kind=kLoop, calls=%fused_computation.1 | loop fusion | flops 983040 | bytes 3538944 | tf_op jit(solution)/shard_map/reduce_sum | solution.py:51
  39.9 5.2 %fusion.6 = (f32[128]{0:T(128)S(1)}, f32[128,3]{0,1:T(4,128)S(1)}) fusion(f32[128,3,512]{2,0,1:T(8,128)S(1)} %copy-done.2, s32[512]{0:T(512)S(1)} %get-tuple-element.45, s32[512]{0:T(512)S(1)} %get-tuple-element.46, s32[512]{0:T(512)S(1)} %add_select_fusion.4, bf16[128,3,512]{2,1,0:T(4,128)(2,1)S(1)} %multiply_reduce_fusion, ...), kind=kOutput, calls=%fused_computation.17 | convolution fusion | flops 208207360 | bytes 1189376 | tf_op jit(solution)/shard_map/dot_general | solution.py:52
  45.1 0.1 broadcast_in_dim.13
  45.2 0.1 broadcast_in_dim.14
  45.3 0.1 broadcast_in_dim.15
  45.5 3.9 %collective-permute-start.1 = (f32[3,1,8,128]{3,2,1,0:T(8,128)S(1)}, f32[3,1,8,128]{3,2,1,0:T(8,128)S(1)}, u32[]{:S(2)}, u32[]{:S(2)}) collective-permute-start(f32[3,1,8,128]{3,2,1,0:T(8,128)S(1)} %get-tuple-element.43), channel_id=1, source_target_pairs={{0,16},{1,17},{2,18},{3,19},{4,20},{5,21},{6,22},{7,23},{8,24},{9,... | collective-permute-start | bytes 36872 | tf_op jit(solution)/shard_map/ppermute | solution.py:20
  49.3 1.3 collective-permute-start
  50.6 0.1 collective-permute-done.1
  50.7 4.2 %collective-permute-done = f32[3,1,8,128]{3,2,1,0:T(8,128)S(1)} collective-permute-done((f32[3,1,8,128]{3,2,1,0:T(8,128)S(1)}, f32[3,1,8,128]{3,2,1,0:T(8,128)S(1)}, u32[]{:S(2)}, u32[]{:S(2)}) %collective-permute-start) | collective-permute-done | bytes 12320 | tf_op jit(solution)/shard_map/ppermute | solution.py:23
  55.0 3.5 %collective-permute-start.3 = (f32[3,10,1,128]{3,2,1,0:T(1,128)S(1)}, f32[3,10,1,128]{3,2,1,0:T(1,128)S(1)}, u32[]{:S(2)}, u32[]{:S(2)}) collective-permute-start(f32[3,10,1,128]{3,2,1,0:T(1,128)S(1)} %get-tuple-element.35), channel_id=1, source_target_pairs={{0,4},{4,8},{8,12},{1,5},{5,9},{9,13},{2,6},{6,10},{10,14},{3,7},{... | collective-permute-start | bytes 46088 | tf_op jit(solution)/shard_map/ppermute | solution.py:20
  58.5 1.3 collective-permute-start.2
  59.8 0.1 collective-permute-done.3
  59.9 4.2 %collective-permute-done.2 = f32[3,10,1,128]{3,2,1,0:T(1,128)S(1)} collective-permute-done((f32[3,10,1,128]{3,2,1,0:T(1,128)S(1)}, f32[3,10,1,128]{3,2,1,0:T(1,128)S(1)}, u32[]{:S(2)}, u32[]{:S(2)}) %collective-permute-start.2) | collective-permute-done | bytes 15392 | tf_op jit(solution)/shard_map/ppermute | solution.py:23
  64.1 0.1 fusion.70
  64.3 1.3 collective-permute-start.4
  65.6 3.0 %collective-permute-start.5 = (f32[3,10,10,1]{3,2,1,0:T(8,128)S(1)}, f32[3,10,10,1]{3,2,1,0:T(8,128)S(1)}, u32[]{:S(2)}, u32[]{:S(2)}) collective-permute-start(f32[3,10,10,1]{3,2,1,0:T(8,128)S(1)} %get-tuple-element.30), channel_id=1, source_target_pairs={{0,1},{1,2},{2,3},{4,5},{5,6},{6,7},{8,9},{9,10},{10,11},{12,13},{... | collective-permute-start | bytes 3608 | tf_op jit(solution)/shard_map/ppermute | solution.py:20
  68.8 0.1 add.235
  68.9 0.8 collective-permute-done.5
  69.7 0.8 multiply_reduce_fusion.7
  70.5 33.2 %all-reduce.2 = (f32[]{:T(128)}, f32[]{:T(128)}) all-reduce(f32[]{:T(128)} %get-tuple-element.9, f32[]{:T(128)} %get-tuple-element.8), channel_id=1, replica_groups=mesh['gx'=2,'gy'=4,'gz'=4] {'gy','gz'}, use_global_device_ids=true, to_apply=%region_4.5 | all-reduce | flops 2 | bytes 16 | tf_op jit(solution)/shard_map/psum | solution.py:80
  103.8 5.5 %all-reduce.5 = (f32[]{:T(128)}, f32[]{:T(128)}) all-reduce(f32[]{:T(128)} %get-tuple-element.14, f32[]{:T(128)} %get-tuple-element.15), channel_id=1, replica_groups=mesh['gx'=2,'gy'=4,'gz'=4] {'gx'}, use_global_device_ids=true, to_apply=%region_5.6 | all-reduce | flops 2 | bytes 16 | tf_op jit(solution)/shard_map/psum | solution.py:79
  110.7 1.9 collective-permute-start.7
  112.6 1.3 collective-permute-start.6
  113.9 0.1 collective-permute-done.7
  114.0 4.2 %collective-permute-done.6 = f32[3,1,8,128]{3,2,1,0:T(8,128)S(1)} collective-permute-done((f32[3,1,8,128]{3,2,1,0:T(8,128)S(1)}, f32[3,1,8,128]{3,2,1,0:T(8,128)S(1)}, u32[]{:S(2)}, u32[]{:S(2)}) %collective-permute-start.6) | collective-permute-done | bytes 12320 | tf_op jit(solution)/shard_map/ppermute | solution.py:23
  118.2 1.3 collective-permute-start.9
  119.5 1.3 collective-permute-start.8
  120.8 0.1 collective-permute-done.9
  120.9 4.2 %collective-permute-done.8 = f32[3,10,1,128]{3,2,1,0:T(1,128)S(1)} collective-permute-done((f32[3,10,1,128]{3,2,1,0:T(1,128)S(1)}, f32[3,10,1,128]{3,2,1,0:T(1,128)S(1)}, u32[]{:S(2)}, u32[]{:S(2)}) %collective-permute-start.8) | collective-permute-done | bytes 15392 | tf_op jit(solution)/shard_map/ppermute | solution.py:23
  125.2 0.1 fusion.69
  125.3 1.3 collective-permute-start.10
  126.6 3.0 %collective-permute-start.11 = (f32[3,10,10,1]{3,2,1,0:T(8,128)S(1)}, f32[3,10,10,1]{3,2,1,0:T(8,128)S(1)}, u32[]{:S(2)}, u32[]{:S(2)}) collective-permute-start(f32[3,10,10,1]{3,2,1,0:T(8,128)S(1)} %get-tuple-element.28), channel_id=1, source_target_pairs={{0,1},{1,2},{2,3},{4,5},{5,6},{6,7},{8,9},{9,10},{10,11},{12,13},{... | collective-permute-start | bytes 3608 | tf_op jit(solution)/shard_map/ppermute | solution.py:20
  129.7 1.1 collective-permute-done.11
  130.8 0.9 multiply_reduce_fusion.5
  131.6 32.2 %all-reduce.1 = (f32[]{:T(128)}, f32[]{:T(128)}) all-reduce(f32[]{:T(128)} %get-tuple-element.7, f32[]{:T(128)} %get-tuple-element.6), channel_id=1, replica_groups=mesh['gx'=2,'gy'=4,'gz'=4] {'gy','gz'}, use_global_device_ids=true, to_apply=%region_11.12 | all-reduce | flops 2 | bytes 16 | tf_op jit(solution)/shard_map/psum | solution.py:80
  163.8 5.6 %all-reduce.4 = (f32[]{:T(128)}, f32[]{:T(128)}) all-reduce(f32[]{:T(128)} %get-tuple-element.12, f32[]{:T(128)} %get-tuple-element.13), channel_id=1, replica_groups=mesh['gx'=2,'gy'=4,'gz'=4] {'gx'}, use_global_device_ids=true, to_apply=%region_12.13 | all-reduce | flops 2 | bytes 16 | tf_op jit(solution)/shard_map/psum | solution.py:79
  174.1 1.9 collective-permute-start.13
  176.0 1.3 collective-permute-start.12
  177.3 0.1 collective-permute-done.13
  177.3 4.2 %collective-permute-done.12 = f32[3,1,8,128]{3,2,1,0:T(8,128)S(1)} collective-permute-done((f32[3,1,8,128]{3,2,1,0:T(8,128)S(1)}, f32[3,1,8,128]{3,2,1,0:T(8,128)S(1)}, u32[]{:S(2)}, u32[]{:S(2)}) %collective-permute-start.12) | collective-permute-done | bytes 12320 | tf_op jit(solution)/shard_map/ppermute | solution.py:23
  181.6 1.3 collective-permute-start.15
  182.9 1.3 collective-permute-start.14
  184.2 0.1 collective-permute-done.15
  184.3 4.2 %collective-permute-done.14 = f32[3,10,1,128]{3,2,1,0:T(1,128)S(1)} collective-permute-done((f32[3,10,1,128]{3,2,1,0:T(1,128)S(1)}, f32[3,10,1,128]{3,2,1,0:T(1,128)S(1)}, u32[]{:S(2)}, u32[]{:S(2)}) %collective-permute-start.14) | collective-permute-done | bytes 15392 | tf_op jit(solution)/shard_map/ppermute | solution.py:23
  188.5 0.1 fusion.68
  188.7 1.3 collective-permute-start.16
  190.0 3.0 %collective-permute-start.17 = (f32[3,10,10,1]{3,2,1,0:T(8,128)S(1)}, f32[3,10,10,1]{3,2,1,0:T(8,128)S(1)}, u32[]{:S(2)}, u32[]{:S(2)}) collective-permute-start(f32[3,10,10,1]{3,2,1,0:T(8,128)S(1)} %get-tuple-element.26), channel_id=1, source_target_pairs={{0,1},{1,2},{2,3},{4,5},{5,6},{6,7},{8,9},{9,10},{10,11},{12,13},{... | collective-permute-start | bytes 3608 | tf_op jit(solution)/shard_map/ppermute | solution.py:20
  193.0 1.1 collective-permute-done.17
  194.1 0.8 multiply_reduce_fusion.3
  194.9 32.1 %all-reduce = (f32[]{:T(128)}, f32[]{:T(128)}) all-reduce(f32[]{:T(128)} %get-tuple-element.5, f32[]{:T(128)} %get-tuple-element.4), channel_id=1, replica_groups=mesh['gx'=2,'gy'=4,'gz'=4] {'gy','gz'}, use_global_device_ids=true, to_apply=%region_17.18 | all-reduce | flops 2 | bytes 16 | tf_op jit(solution)/shard_map/psum | solution.py:80
  227.1 5.5 %all-reduce.3 = (f32[]{:T(128)}, f32[]{:T(128)}) all-reduce(f32[]{:T(128)} %get-tuple-element.10, f32[]{:T(128)} %get-tuple-element.11), channel_id=1, replica_groups=mesh['gx'=2,'gy'=4,'gz'=4] {'gx'}, use_global_device_ids=true, to_apply=%region_18.19 | all-reduce | flops 2 | bytes 16 | tf_op jit(solution)/shard_map/psum | solution.py:79
  236.6 0.7 multiply_subtract_fusion
  (28 shorter events, 0.5 us)
Async XLA Ops:
  9.7 4.8 %copy-start.1 = (f32[128,3,512]{2,0,1:T(8,128)}, f32[128,3,512]{2,0,1:T(8,128)S(1)}, u32[]{:S(2)}) copy-start(f32[128,3,512]{2,0,1:T(8,128)S(1)} %copy.35) | copy-start | bytes 2359300
  34.7 5.2 %copy-start.2 = (f32[128,3,512]{2,0,1:T(8,128)S(1)}, f32[128,3,512]{2,0,1:T(8,128)}, u32[]{:S(2)}) copy-start(f32[128,3,512]{2,0,1:T(8,128)} %copy-done.1) | copy-start | bytes 2359300
  39.9 5.5 %copy-start = (f32[3,8,8,128]{3,2,1,0:T(8,128)S(1)}, f32[3,8,8,128]{3,2,1,0:T(8,128)}, u32[]{:S(2)}) copy-start(f32[3,8,8,128]{3,2,1,0:T(8,128)} %param.6) | copy-start | bytes 294916
  45.5 5.3 %collective-permute-start.1 = (f32[3,1,8,128]{3,2,1,0:T(8,128)S(1)}, f32[3,1,8,128]{3,2,1,0:T(8,128)S(1)}, u32[]{:S(2)}, u32[]{:S(2)}) collective-permute-start(f32[3,1,8,128]{3,2,1,0:T(8,128)S(1)} %get-tuple-element.43), channel_id=1, source_target_pairs={{0,16},{1,17},{2,18},{3,19},{4,20},{5,21},{6,22},{7,23},{8,24},{9,... | collective-permute-start | bytes 36872 | tf_op jit(solution)/shard_map/ppermute | solution.py:20
  49.3 5.6 %collective-permute-start = (f32[3,1,8,128]{3,2,1,0:T(8,128)S(1)}, f32[3,1,8,128]{3,2,1,0:T(8,128)S(1)}, u32[]{:S(2)}, u32[]{:S(2)}) collective-permute-start(f32[3,1,8,128]{3,2,1,0:T(8,128)S(1)} %get-tuple-element.44), channel_id=1, source_target_pairs={{16,0},{17,1},{18,2},{19,3},{20,4},{21,5},{22,6},{23,7},{24,8},{25... | collective-permute-start | bytes 36872 | tf_op jit(solution)/shard_map/ppermute | solution.py:23
  55.0 4.9 %collective-permute-start.3 = (f32[3,10,1,128]{3,2,1,0:T(1,128)S(1)}, f32[3,10,1,128]{3,2,1,0:T(1,128)S(1)}, u32[]{:S(2)}, u32[]{:S(2)}) collective-permute-start(f32[3,10,1,128]{3,2,1,0:T(1,128)S(1)} %get-tuple-element.35), channel_id=1, source_target_pairs={{0,4},{4,8},{8,12},{1,5},{5,9},{9,13},{2,6},{6,10},{10,14},{3,7},{... | collective-permute-start | bytes 46088 | tf_op jit(solution)/shard_map/ppermute | solution.py:20
  58.5 5.6 %collective-permute-start.2 = (f32[3,10,1,128]{3,2,1,0:T(1,128)S(1)}, f32[3,10,1,128]{3,2,1,0:T(1,128)S(1)}, u32[]{:S(2)}, u32[]{:S(2)}) collective-permute-start(f32[3,10,1,128]{3,2,1,0:T(1,128)S(1)} %get-tuple-element.36), channel_id=1, source_target_pairs={{4,0},{8,4},{12,8},{5,1},{9,5},{13,9},{6,2},{10,6},{14,10},{7,3},{... | collective-permute-start | bytes 46088 | tf_op jit(solution)/shard_map/ppermute | solution.py:23
  64.3 4.6 %collective-permute-start.4 = (f32[3,10,10,1]{3,2,1,0:T(8,128)S(1)}, f32[3,10,10,1]{3,2,1,0:T(8,128)S(1)}, u32[]{:S(2)}, u32[]{:S(2)}) collective-permute-start(f32[3,10,10,1]{3,2,1,0:T(8,128)S(1)} %get-tuple-element.29), channel_id=1, source_target_pairs={{1,0},{2,1},{3,2},{5,4},{6,5},{7,6},{9,8},{10,9},{11,10},{13,12},{... | collective-permute-start | bytes 3608 | tf_op jit(solution)/shard_map/ppermute | solution.py:23
  65.6 4.2 %collective-permute-start.5 = (f32[3,10,10,1]{3,2,1,0:T(8,128)S(1)}, f32[3,10,10,1]{3,2,1,0:T(8,128)S(1)}, u32[]{:S(2)}, u32[]{:S(2)}) collective-permute-start(f32[3,10,10,1]{3,2,1,0:T(8,128)S(1)} %get-tuple-element.30), channel_id=1, source_target_pairs={{0,1},{1,2},{2,3},{4,5},{5,6},{6,7},{8,9},{9,10},{10,11},{12,13},{... | collective-permute-start | bytes 3608 | tf_op jit(solution)/shard_map/ppermute | solution.py:20
  110.7 3.3 %collective-permute-start.7 = (f32[3,1,8,128]{3,2,1,0:T(8,128)S(1)}, f32[3,1,8,128]{3,2,1,0:T(8,128)S(1)}, u32[]{:S(2)}, u32[]{:S(2)}) collective-permute-start(f32[3,1,8,128]{3,2,1,0:T(8,128)S(1)} %get-tuple-element.41), channel_id=1, source_target_pairs={{0,16},{1,17},{2,18},{3,19},{4,20},{5,21},{6,22},{7,23},{8,24},{9,... | collective-permute-start | bytes 36872 | tf_op jit(solution)/shard_map/ppermute | solution.py:20
  112.6 5.6 %collective-permute-start.6 = (f32[3,1,8,128]{3,2,1,0:T(8,128)S(1)}, f32[3,1,8,128]{3,2,1,0:T(8,128)S(1)}, u32[]{:S(2)}, u32[]{:S(2)}) collective-permute-start(f32[3,1,8,128]{3,2,1,0:T(8,128)S(1)} %get-tuple-element.42), channel_id=1, source_target_pairs={{16,0},{17,1},{18,2},{19,3},{20,4},{21,5},{22,6},{23,7},{24,8},{25... | collective-permute-start | bytes 36872 | tf_op jit(solution)/shard_map/ppermute | solution.py:23
  118.2 2.7 %collective-permute-start.9 = (f32[3,10,1,128]{3,2,1,0:T(1,128)S(1)}, f32[3,10,1,128]{3,2,1,0:T(1,128)S(1)}, u32[]{:S(2)}, u32[]{:S(2)}) collective-permute-start(f32[3,10,1,128]{3,2,1,0:T(1,128)S(1)} %get-tuple-element.33), channel_id=1, source_target_pairs={{0,4},{4,8},{8,12},{1,5},{5,9},{9,13},{2,6},{6,10},{10,14},{3,7},{... | collective-permute-start | bytes 46088 | tf_op jit(solution)/shard_map/ppermute | solution.py:20
  119.5 5.6 %collective-permute-start.8 = (f32[3,10,1,128]{3,2,1,0:T(1,128)S(1)}, f32[3,10,1,128]{3,2,1,0:T(1,128)S(1)}, u32[]{:S(2)}, u32[]{:S(2)}) collective-permute-start(f32[3,10,1,128]{3,2,1,0:T(1,128)S(1)} %get-tuple-element.34), channel_id=1, source_target_pairs={{4,0},{8,4},{12,8},{5,1},{9,5},{13,9},{6,2},{10,6},{14,10},{7,3},{... | collective-permute-start | bytes 46088 | tf_op jit(solution)/shard_map/ppermute | solution.py:23
  125.3 4.4 %collective-permute-start.10 = (f32[3,10,10,1]{3,2,1,0:T(8,128)S(1)}, f32[3,10,10,1]{3,2,1,0:T(8,128)S(1)}, u32[]{:S(2)}, u32[]{:S(2)}) collective-permute-start(f32[3,10,10,1]{3,2,1,0:T(8,128)S(1)} %get-tuple-element.27), channel_id=1, source_target_pairs={{1,0},{2,1},{3,2},{5,4},{6,5},{7,6},{9,8},{10,9},{11,10},{13,12},{... | collective-permute-start | bytes 3608 | tf_op jit(solution)/shard_map/ppermute | solution.py:23
  126.6 4.2 %collective-permute-start.11 = (f32[3,10,10,1]{3,2,1,0:T(8,128)S(1)}, f32[3,10,10,1]{3,2,1,0:T(8,128)S(1)}, u32[]{:S(2)}, u32[]{:S(2)}) collective-permute-start(f32[3,10,10,1]{3,2,1,0:T(8,128)S(1)} %get-tuple-element.28), channel_id=1, source_target_pairs={{0,1},{1,2},{2,3},{4,5},{5,6},{6,7},{8,9},{9,10},{10,11},{12,13},{... | collective-permute-start | bytes 3608 | tf_op jit(solution)/shard_map/ppermute | solution.py:20
  174.1 3.3 %collective-permute-start.13 = (f32[3,1,8,128]{3,2,1,0:T(8,128)S(1)}, f32[3,1,8,128]{3,2,1,0:T(8,128)S(1)}, u32[]{:S(2)}, u32[]{:S(2)}) collective-permute-start(f32[3,1,8,128]{3,2,1,0:T(8,128)S(1)} %get-tuple-element.39), channel_id=1, source_target_pairs={{0,16},{1,17},{2,18},{3,19},{4,20},{5,21},{6,22},{7,23},{8,24},{9,... | collective-permute-start | bytes 36872 | tf_op jit(solution)/shard_map/ppermute | solution.py:20
  176.0 5.6 %collective-permute-start.12 = (f32[3,1,8,128]{3,2,1,0:T(8,128)S(1)}, f32[3,1,8,128]{3,2,1,0:T(8,128)S(1)}, u32[]{:S(2)}, u32[]{:S(2)}) collective-permute-start(f32[3,1,8,128]{3,2,1,0:T(8,128)S(1)} %get-tuple-element.40), channel_id=1, source_target_pairs={{16,0},{17,1},{18,2},{19,3},{20,4},{21,5},{22,6},{23,7},{24,8},{25... | collective-permute-start | bytes 36872 | tf_op jit(solution)/shard_map/ppermute | solution.py:23
  181.6 2.7 %collective-permute-start.15 = (f32[3,10,1,128]{3,2,1,0:T(1,128)S(1)}, f32[3,10,1,128]{3,2,1,0:T(1,128)S(1)}, u32[]{:S(2)}, u32[]{:S(2)}) collective-permute-start(f32[3,10,1,128]{3,2,1,0:T(1,128)S(1)} %get-tuple-element.31), channel_id=1, source_target_pairs={{0,4},{4,8},{8,12},{1,5},{5,9},{9,13},{2,6},{6,10},{10,14},{3,7},{... | collective-permute-start | bytes 46088 | tf_op jit(solution)/shard_map/ppermute | solution.py:20
  182.9 5.6 %collective-permute-start.14 = (f32[3,10,1,128]{3,2,1,0:T(1,128)S(1)}, f32[3,10,1,128]{3,2,1,0:T(1,128)S(1)}, u32[]{:S(2)}, u32[]{:S(2)}) collective-permute-start(f32[3,10,1,128]{3,2,1,0:T(1,128)S(1)} %get-tuple-element.32), channel_id=1, source_target_pairs={{4,0},{8,4},{12,8},{5,1},{9,5},{13,9},{6,2},{10,6},{14,10},{7,3},{... | collective-permute-start | bytes 46088 | tf_op jit(solution)/shard_map/ppermute | solution.py:23
  188.7 4.4 %collective-permute-start.16 = (f32[3,10,10,1]{3,2,1,0:T(8,128)S(1)}, f32[3,10,10,1]{3,2,1,0:T(8,128)S(1)}, u32[]{:S(2)}, u32[]{:S(2)}) collective-permute-start(f32[3,10,10,1]{3,2,1,0:T(8,128)S(1)} %get-tuple-element.25), channel_id=1, source_target_pairs={{1,0},{2,1},{3,2},{5,4},{6,5},{7,6},{9,8},{10,9},{11,10},{13,12},{... | collective-permute-start | bytes 3608 | tf_op jit(solution)/shard_map/ppermute | solution.py:23
  190.0 4.2 %collective-permute-start.17 = (f32[3,10,10,1]{3,2,1,0:T(8,128)S(1)}, f32[3,10,10,1]{3,2,1,0:T(8,128)S(1)}, u32[]{:S(2)}, u32[]{:S(2)}) collective-permute-start(f32[3,10,10,1]{3,2,1,0:T(8,128)S(1)} %get-tuple-element.26), channel_id=1, source_target_pairs={{0,1},{1,2},{2,3},{4,5},{5,6},{6,7},{8,9},{9,10},{10,11},{12,13},{... | collective-permute-start | bytes 3608 | tf_op jit(solution)/shard_map/ppermute | solution.py:20
